TPU v7x, 256 devices: a whole 4x4x8 slice. The times are simulated.
256 devices in a mesh: lat: 4 (over x), lon: 2 (over core), ens: 32 (over z, y).
Axes of the slice: x: 4, y: 4, z: 8, core: 2. Of those that a mesh axis runs over, the one named last changes fastest.
Arguments:
- inputs: bfloat16 [32, 8, 1440, 256], P('ens', 'lat', 'lon'), may hold values from -12 to 12
- weight: bfloat16 [9, 256, 256], replicated, may hold values from -0.125 to 0.125
- spread: int32 [8], P('lat'), may hold values from 2 to 16, as said below
- target: bfloat16 [8, 1440, 256], P('lat', 'lon'), may hold values from -6 to 6
Outputs:
- response: bfloat16 [32, 8, 1440, 256], P('ens', 'lat', 'lon')
- grad_input: bfloat16 [32, 8, 1440, 256], P('ens', 'lat', 'lon')
- grad_weight: float32 [9, 256, 256], replicated
- loss: float32 [], replicated
Inputs may be any that keep to these rules, and one draw needn't show every extreme that they name: The filter of row o spans 2 spread[o] + 1 longitudes; spread is 16 on the 2 polar rows at each pole, which ignore it, and on the next row toward the equator.
All inputs are finite; a program needn't handle non-finite values.
Results may differ from a plain program's by a relative error of at most 0.009.
Values may be sent and summed in bfloat16 or wider, within the bound.
No kernel may reach another device: no remote copies, remote signals or barrier semaphores. Data moves between devices by JAX's collectives and lax.ppermute only.
A program may use at most 128 MiB of HBM per device.

v0:
```python
import math
import jax
import jax.numpy as jnp
from jax import lax
from jax.sharding import PartitionSpec as P

PCAP = 2
HMAX = 16
highest = lax.Precision.HIGHEST


def extended_2(block, sides, width):
    for axis, dim in sides:
        count = lax.axis_size(axis)
        forward = [(i, i + 1) for i in range(count - 1)]
        backward = [(target, source) for source, target in forward]
        low = lax.ppermute(
            lax.slice_in_dim(block, block.shape[dim] - width, None, axis=dim), axis, forward
        )
        high = lax.ppermute(lax.slice_in_dim(block, 0, width, axis=dim), axis, backward)
        block = jnp.concatenate([low, block, high], axis=dim)
    return block


def kernel_rows(spread_rows, lon_count, reach):
    halves = spread_rows.astype(jnp.float32)[:, None, None, None] / 2.0
    columns = jnp.arange(lon_count)
    window_cols = jnp.arange(lon_count + 2 * reach)
    offsets = (window_cols[None, :] - reach - columns[:, None]).astype(jnp.float32)
    centres = (jnp.arange(3) - 1).astype(jnp.float32)[None, :, None, None] * halves
    values = jnp.maximum(0.0, 1.0 - jnp.abs(offsets[None, None] - centres) / halves) / halves
    return values.astype(jnp.bfloat16)


def circle_basis(first_col, lon_count, circle):
    angles = 2.0 * math.pi * (first_col + jnp.arange(lon_count)).astype(jnp.float32) / circle
    return jnp.stack([jnp.ones_like(angles), jnp.cos(angles), jnp.sin(angles)])


def circular(circle_sums, basis, circle, row_count):
    cos_wave = basis[1][None, None, :, None]
    sin_wave = basis[2][None, None, :, None]
    pieces = []
    for lat_tap in range(3):
        tap_sums = circle_sums[:, :, lat_tap : lat_tap + row_count]
        mean_part = tap_sums[:, 0][:, :, None, :] / circle
        cosine_part = (
            2.0
            / circle
            * (cos_wave * tap_sums[:, 1][:, :, None, :] + sin_wave * tap_sums[:, 2][:, :, None, :])
        )
        sine_part = (
            2.0
            / circle
            * (cos_wave * tap_sums[:, 2][:, :, None, :] - sin_wave * tap_sums[:, 1][:, :, None, :])
        )
        pieces += [jnp.broadcast_to(mean_part, cosine_part.shape), cosine_part, sine_part]
    return jnp.stack(pieces, 2)


def crps_terms(values, every_member, truth, lat_weight, member_total):
    miss = values - truth
    own_dist = jnp.sqrt(miss * miss + 0.25)
    own_slope = miss / own_dist

    def add_member(member, carry):
        pair_dist, pair_slope = carry
        other = lax.dynamic_index_in_dim(every_member, member, 0, keepdims=True).astype(jnp.float32)
        gap_value = values - other
        distance = jnp.sqrt(gap_value * gap_value + 0.25)
        return (pair_dist + distance, pair_slope + gap_value / distance)

    start = (jnp.zeros_like(values), jnp.zeros_like(values))
    pair_dist, pair_slope = lax.fori_loop(0, member_total, add_member, start)
    pair_dist = pair_dist - 0.5
    scores = own_dist / member_total - pair_dist / (2 * member_total * (member_total - 1))
    weighted = jnp.sum(lat_weight * scores)
    slopes = (
        lat_weight * (own_slope / member_total - pair_slope / (member_total * (member_total - 1)))
    ).astype(jnp.bfloat16)
    return (weighted, slopes)


def per_device(inputs, weight, spread, target):
    ens_local, row_count, lon_count, channels = inputs.shape
    reach = HMAX
    lat_total = row_count * lax.axis_size("lat")
    lon_total = lon_count * lax.axis_size("lon")
    lon_first = lax.axis_index("lon") * lon_count
    global_rows = lax.axis_index("lat") * row_count + jnp.arange(row_count)
    polar_rows = (global_rows < PCAP) | (global_rows >= lat_total - PCAP)
    polar_mask = polar_rows[None, :, None, None, None]
    kernels = kernel_rows(spread, lon_count, reach)
    local_basis = circle_basis(lon_first, lon_count, lon_total)
    extended = extended_2(inputs, (("lat", 1),), 1)
    whole_circle = lax.all_gather(extended, "lon", axis=2, tiled=True)
    window_start = (lon_first - reach + lon_total) % lon_total
    doubled = jnp.concatenate([whole_circle, whole_circle], 2)
    window = lax.dynamic_slice_in_dim(doubled, window_start, lon_count + 2 * reach, 2)
    full_basis = circle_basis(0, lon_total, lon_total)
    circle_sums = jnp.einsum(
        "pj,erjc->eprc", full_basis, whole_circle.astype(jnp.float32), precision=highest
    )
    banded = jnp.concatenate(
        [
            jnp.einsum(
                "objq,eoqc->eobjc",
                kernels,
                window[:, lat_tap : lat_tap + row_count],
                preferred_element_type=jnp.float32,
            )
            for lat_tap in range(3)
        ],
        2,
    )
    rounds = circular(circle_sums, local_basis, lon_total, row_count)
    features = jnp.where(polar_mask, rounds, banded).astype(jnp.bfloat16)
    response = jnp.einsum(
        "eokjc,kcd->eojd", features, weight, preferred_element_type=jnp.float32
    ).astype(jnp.bfloat16)
    member_total = ens_local * lax.axis_size("ens")
    row_weight = jnp.sin(math.pi * (global_rows.astype(jnp.float32) + 0.5) / lat_total)
    ensemble = lax.all_gather(response, "ens", axis=0, tiled=True)
    truth = target.astype(jnp.float32)[None]
    weighted, slopes = crps_terms(
        response.astype(jnp.float32), ensemble, truth, row_weight[None, :, None, None], member_total
    )
    loss_part = weighted / (lat_total * lon_total * channels)
    weight_part = jnp.einsum(
        "eokjc,eojd->kcd", features, slopes, preferred_element_type=jnp.float32
    )
    weight_sum, loss = lax.psum((weight_part, loss_part), ("lat", "lon", "ens"))
    grad_weight = weight_sum * math.sqrt(weight.shape[0] * channels) / (lat_total * lon_total)
    feature_grad = jnp.einsum(
        "eojd,kcd->eokjc", slopes, weight, preferred_element_type=jnp.float32
    ).astype(jnp.bfloat16)
    zero_grad = jnp.zeros_like(feature_grad)
    band_grad = jnp.where(polar_mask, zero_grad, feature_grad)
    circle_grad = jnp.where(polar_mask, feature_grad, zero_grad)
    window_grad = jnp.zeros(
        (ens_local, row_count + 2, lon_count + 2 * reach, channels), jnp.float32
    )
    sum_grad = jnp.zeros((ens_local, 3, row_count + 2, channels), jnp.float32)
    cos_wave = local_basis[1]
    sin_wave = local_basis[2]
    for lat_tap in range(3):
        picked = band_grad[:, :, 3 * lat_tap : 3 * lat_tap + 3]
        window_grad = window_grad.at[:, lat_tap : lat_tap + row_count].add(
            jnp.einsum("objq,eobjc->eoqc", kernels, picked, preferred_element_type=jnp.float32)
        )
        tap_grad = circle_grad[:, :, 3 * lat_tap : 3 * lat_tap + 3].astype(jnp.float32)
        mean_grad = jnp.sum(tap_grad[:, :, 0], axis=2) / lon_total
        cos_grad = (
            2.0
            / lon_total
            * (
                jnp.einsum("j,eojc->eoc", cos_wave, tap_grad[:, :, 1], precision=highest)
                - jnp.einsum("j,eojc->eoc", sin_wave, tap_grad[:, :, 2], precision=highest)
            )
        )
        sin_grad = (
            2.0
            / lon_total
            * (
                jnp.einsum("j,eojc->eoc", sin_wave, tap_grad[:, :, 1], precision=highest)
                + jnp.einsum("j,eojc->eoc", cos_wave, tap_grad[:, :, 2], precision=highest)
            )
        )
        sum_grad = sum_grad.at[:, :, lat_tap : lat_tap + row_count].add(
            jnp.stack([mean_grad, cos_grad, sin_grad], 1)
        )
    spread_back = jnp.einsum("pj,eprc->erjc", full_basis, sum_grad, precision=highest)
    placed = jnp.zeros((ens_local, row_count + 2, 2 * lon_total, channels), jnp.float32)
    placed = lax.dynamic_update_slice_in_dim(placed, window_grad, window_start, 2)
    spread_back = spread_back + placed[:, :, :lon_total] + placed[:, :, lon_total:]
    core = lax.psum_scatter(
        spread_back.astype(jnp.bfloat16), "lon", scatter_dimension=2, tiled=True
    ).astype(jnp.float32)
    edges = jnp.concatenate([core[:, :1], core[:, row_count + 1 :]], 1)
    arrived_rows = extended_2(edges.astype(jnp.bfloat16), (("lat", 1),), 1).astype(edges.dtype)
    inner = core[:, 1 : row_count + 1]
    inner = inner.at[:, 0].add(arrived_rows[:, 0])
    inner = inner.at[:, row_count - 1].add(arrived_rows[:, 3])
    return (response, inner.astype(jnp.bfloat16), grad_weight, loss)


def solution(mesh):
    in_specs = (P("ens", "lat", "lon", None), P(), P("lat"), P("lat", "lon", None))
    out_specs = (P("ens", "lat", "lon", None), P("ens", "lat", "lon", None), P(), P())
    return jax.shard_map(
        per_device, mesh=mesh, in_specs=in_specs, out_specs=out_specs, check_vma=False
    )
```

profile of v0, /device:TPU:2, one launch (start us, length us, event | category | flops | bytes accessed | tf_op | source)
XLA Modules:
  0.0 740.7 jit_solution(5865980801284775677)
XLA Ops:
  14.4 6.3 collective-permute-done
  27.0 19.3 %all-gather.4.cloned.1.call-done = bf16[1,4,1440,256]{3,2,1,0:T(8,128)(2,1)} async-done(((bf16[1,4,720,256]{3,2,1,0:T(8,128)(2,1)}), bf16[1,4,1440,256]{3,2,1,0:T(8,128)(2,1)}) %all-gather.4.cloned.1.call-update) | async-done | bytes 2949136 | tf_op jit(solution)/shard_map/all_gather | solution.py:96
  71.5 174.4 %all-gather.6.cloned.1.call-done = bf16[64,720,256]{2,1,0:T(8,128)(2,1)} async-done(((bf16[2,720,256]{2,1,0:T(8,128)(2,1)}), bf16[64,720,256]{2,1,0:T(8,128)(2,1)}) %all-gather.6.cloned.1.call-update) | async-done | bytes 23592976 | tf_op jit(solution)/shard_map/all_gather | solution.py:123
  245.9 140.6 %while.24 = (s32[]{:T(128)}, f32[1,2,720,256]{3,2,1,0:T(8,128)}, f32[1,2,720,256]{3,2,1,0:T(8,128)}, bf16[32,2,720,256]{3,2,1,0:T(8,128)(2,1)}, f32[1,2,720,256]{3,2,1,0:T(8,128)S(1)}, /*index=5*/s32[]{:T(128)}, s32[]{:T(128)}) while((s32[]{:T(128)}, f32[1,2,720,256]{3,2,1,0:T(8,128)}, f32[1,2,720,256]{3,2,1,0:T(8,128)}, ...), condition=%wide.region_1.2_spmd.clone, body=%wide.region_0.1_spmd.clone.sunk | while | flops 3317763 | bytes 8110179 | solution.py:74
  249.5 4.4 select_add_fusion.3
  253.9 4.4 select_add_fusion.3
  258.3 4.4 select_add_fusion.3
  262.7 4.4 select_add_fusion.3
  267.2 4.4 select_add_fusion.3
  271.6 4.4 select_add_fusion.3
  276.0 4.4 select_add_fusion.3
  280.4 4.4 select_add_fusion.3
  284.8 4.4 select_add_fusion.3
  289.3 4.4 select_add_fusion.3
  293.7 4.4 select_add_fusion.3
  298.1 4.4 select_add_fusion.3
  302.5 4.4 select_add_fusion.3
  306.9 4.4 select_add_fusion.3
  315.8 4.4 select_add_fusion.3
  329.0 4.4 select_add_fusion.3
  351.2 4.4 select_add_fusion.3
  364.4 4.4 select_add_fusion.3
  377.7 4.4 select_add_fusion.3
  399.8 5.7 fusion.12
  407.4 6.8 fusion.11
  414.2 6.8 fusion.10
  420.9 5.4 broadcast_in_dim.38
  426.3 8.8 %dynamic_update_slice.3 = f32[1,4,2880,256]{3,2,1,0:T(8,128)} dynamic-update-slice(f32[1,4,2880,256]{3,2,1,0:T(8,128)} %broadcast_in_dim.38, f32[1,4,752,256]{3,2,1,0:T(8,128)} %fusion.10, s32[]{:T(128)} %constant.322.clone.1, s32[]{:T(128)} %constant.322.clone.1, s32[]{:T(128)S(6)} %select_n.39, s32[]{:T(128)} %constant.322.clone.1) | dynamic-update-slice | bytes 6160388 | tf_op jit(solution)/shard_map/dynamic_update_slice | solution.py:174
  435.2 9.4 %fusion.3 = bf16[1,4,1440,256]{3,2,1,0:T(8,128)(2,1)} fusion(f32[1,4,2880,256]{3,2,1,0:T(8,128)} %dynamic_update_slice.3, f32[3,4,256]{2,0,1:T(4,128)S(1)} %fusion.41, f32[1,1440]{1,0:T(1,128)S(1)} %copy-done.11, f32[1,1440]{1,0:T(1,128)S(1)} %copy-done.13, f32[3]{0:T(128)S(1)} %copy-done.15), kind=kOutput, calls=%fused_computation.12 | convolution fusion | flops 57516480 | bytes 14769420 | tf_op jit(solution)/shard_map/pj,eprc->erjc/dot_general | solution.py:172
  445.7 6.4 convolution_bitcast_fusion.3
  452.8 73.8 %psum.15 = f32[]{:T(128)} all-reduce(f32[]{:T(128)S(6)} %div.141), channel_id=1, replica_groups=mesh['lat'=4,'lon'=2,'ens'=32] {'lat','lon','ens'}, use_global_device_ids=true, to_apply=%region_8.9 | all-reduce | flops 1 | bytes 8 | tf_op jit(solution)/shard_map/psum | solution.py:132
  533.8 195.4 %all-reduce.4.cloned.1.call-done = f32[9,256,256]{2,1,0:T(8,128)} async-done(((f32[9,256,256]{2,1,0:T(8,128)}), f32[9,256,256]{2,1,0:T(8,128)}) %all-reduce.4.cloned.1.call-update) | async-done | bytes 2359312 | tf_op jit(solution)/shard_map/psum | solution.py:132
  (149 shorter events, 123.2 us)
Async XLA Ops:
  7.2 60.0 %copy-start = (bf16[9,256,256]{2,1,0:T(8,128)(2,1)S(1)}, bf16[9,256,256]{2,1,0:T(8,128)(2,1)}, u32[]{:S(2)}) copy-start(bf16[9,256,256]{2,1,0:T(8,128)(2,1)} %param.23) | copy-start | bytes 3538948
  7.2 19.3 %copy-start.16 = (s32[2]{0:T(128)S(1)}, s32[2]{0:T(128)}, u32[]{:S(2)}) copy-start(s32[2]{0:T(128)} %param.24) | copy-start | bytes 28
  7.2 39.1 %all-gather.4.cloned.1.call-start = ((), (), s32[]{:S(2)}) async-start(), calls=%async_computation.1 | async-start | bytes 4423680 | tf_op jit(solution)/shard_map/all_gather | solution.py:96
  8.5 12.2 %collective-permute-start = (bf16[1,1,720,256]{3,2,1,0:T(8,128)(2,1)S(1)}, bf16[1,1,720,256]{3,2,1,0:T(8,128)(2,1)S(1)}, u32[]{:S(2)}, u32[]{:S(2)}) collective-permute-start(bf16[1,1,720,256]{3,2,1,0:T(8,128)(2,1)S(1)} %get-tuple-element.236), channel_id=1, source_target_pairs={{0,64},{64,128},{128,192},{1,65},{65,129},{129,193},{2,66},{66,130... | collective-permute-start | bytes 1105928 | tf_op jit(solution)/shard_map/ppermute | solution.py:17
  11.9 11.9 %collective-permute-start.1 = (bf16[1,1,720,256]{3,2,1,0:T(8,128)(2,1)S(1)}, bf16[1,1,720,256]{3,2,1,0:T(8,128)(2,1)S(1)}, u32[]{:S(2)}, u32[]{:S(2)}) collective-permute-start(bf16[1,1,720,256]{3,2,1,0:T(8,128)(2,1)S(1)} %get-tuple-element.237), channel_id=1, source_target_pairs={{64,0},{128,64},{192,128},{65,1},{129,65},{193,129},{66,2},{130,66... | collective-permute-start | bytes 1105928 | tf_op jit(solution)/shard_map/ppermute | solution.py:20
  26.3 219.6 %all-gather.6.cloned.1.call-start = ((), (), s32[]{:S(2)}) async-start(), calls=%async_computation.4 | async-start | bytes 24330240 | tf_op jit(solution)/shard_map/all_gather | solution.py:123
  26.4 25.0 %copy-start.14 = (f32[3]{0:T(128)}, f32[3]{0:T(128)S(1)}, u32[]{:S(2)}) copy-start(f32[3]{0:T(128)S(1)} %pad.37.clone) | copy-start | bytes 40
  26.7 24.6 %copy-start.10 = (f32[1,1440]{1,0:T(1,128)}, f32[1,1440]{1,0:T(1,128)S(1)}, u32[]{:S(2)}) copy-start(f32[1,1440]{1,0:T(1,128)S(1)} %get-tuple-element.247) | copy-start | bytes 17284
  26.7 24.6 %copy-start.12 = (f32[1,1440]{1,0:T(1,128)}, f32[1,1440]{1,0:T(1,128)S(1)}, u32[]{:S(2)}) copy-start(f32[1,1440]{1,0:T(1,128)S(1)} %get-tuple-element.248) | copy-start | bytes 17284
  27.0 30.9 %copy-start.6 = (f32[720,752]{1,0:T(8,128)}, f32[720,752]{1,0:T(8,128)S(1)}, u32[]{:S(2)}) copy-start(f32[720,752]{1,0:T(8,128)S(1)} %subtract_convert_fusion) | copy-start | bytes 6497284
  46.2 3.3 copy-start.2
  64.3 2.8 copy-start.4
  69.9 456.7 %reduce-scatter.2.cloned.1.call-start = ((), (), s32[]{:S(2)}) async-start(), calls=%async_computation.2 | async-start | bytes 4423680 | tf_op jit(solution)/shard_map/reduce_scatter | solution.py:176
  245.9 140.6 %copy-start.5 = (bf16[2,720,256]{2,1,0:T(8,128)(2,1)S(1)}, bf16[2,720,256]{2,1,0:T(8,128)(2,1)}, u32[]{:S(2)}) copy-start(bf16[2,720,256]{2,1,0:T(8,128)(2,1)} %bitcast_convert_fusion) | copy-start | bytes 2211844
  390.4 3.9 copy-start.8
  397.1 2.7 copy-start.7
  426.3 8.8 %copy-start.11 = (f32[1,1440]{1,0:T(1,128)S(1)}, f32[1,1440]{1,0:T(1,128)}, u32[]{:S(2)}) copy-start(f32[1,1440]{1,0:T(1,128)} %copy-done.10) | copy-start | bytes 17284
  426.3 8.8 %copy-start.13 = (f32[1,1440]{1,0:T(1,128)S(1)}, f32[1,1440]{1,0:T(1,128)}, u32[]{:S(2)}) copy-start(f32[1,1440]{1,0:T(1,128)} %copy-done.12) | copy-start | bytes 17284
  426.3 8.8 %copy-start.15 = (f32[3]{0:T(128)S(1)}, f32[3]{0:T(128)}, u32[]{:S(2)}) copy-start(f32[3]{0:T(128)} %copy-done.14) | copy-start | bytes 40
  444.6 1.1 copy-start.9
  444.6 284.5 %all-reduce.4.cloned.1.call-start = ((), (), s32[]{:S(2)}) async-start(), calls=%async_computation.3 | async-start | bytes 4718592 | tf_op jit(solution)/shard_map/psum | solution.py:132
  526.6 205.8 %copy-start.3 = (bf16[1,4,720,256]{3,2,1,0:T(8,128)(2,1)S(1)}, bf16[1,4,720,256]{3,2,1,0:T(8,128)(2,1)}, u32[]{:S(2)}) copy-start(bf16[1,4,720,256]{3,2,1,0:T(8,128)(2,1)} %reduce-scatter.2.cloned.1.call-done) | copy-start | bytes 4423684
  527.9 205.0 %collective-permute-start.2 = (bf16[1,1,720,256]{3,2,1,0:T(8,128)(2,1)S(1)}, bf16[1,1,720,256]{3,2,1,0:T(8,128)(2,1)S(1)}, u32[]{:S(2)}, u32[]{:S(2)}) collective-permute-start(bf16[1,1,720,256]{3,2,1,0:T(8,128)(2,1)S(1)} %get-tuple-element.234), channel_id=1, source_target_pairs={{0,64},{64,128},{128,192},{1,65},{65,129},{129,193},{2,66},{66,130... | collective-permute-start | bytes 1105928 | tf_op jit(solution)/shard_map/ppermute | solution.py:17
  530.8 202.0 %collective-permute-start.3 = (bf16[1,1,720,256]{3,2,1,0:T(8,128)(2,1)S(1)}, bf16[1,1,720,256]{3,2,1,0:T(8,128)(2,1)S(1)}, u32[]{:S(2)}, u32[]{:S(2)}) collective-permute-start(bf16[1,1,720,256]{3,2,1,0:T(8,128)(2,1)S(1)} %get-tuple-element.235), channel_id=1, source_target_pairs={{64,0},{128,64},{192,128},{65,1},{129,65},{193,129},{66,2},{130,66... | collective-permute-start | bytes 1105928 | tf_op jit(solution)/shard_map/ppermute | solution.py:20
  732.9 1.3 copy-start.1
Sparse Core Ops, SparseCore 0:
  26.4 19.8 all-gather.3
  70.1 175.7 all-gather.5
  444.7 13.3 reduce-scatter.1
  464.0 265.1 all-reduce.3
where the time goes:
time: 742 us; the launch traced here: 741 us
  waiting for transfers between devices  399 us (54%)
  other arithmetic  159 us (21%)
  blocking collectives  73.8 us (10%)
  matrix products  59.5 us (8%)
  local copies, waits for them, and re-layouts  23.1 us (3%)
  between operations  15.1 us (2%)
  starting transfers between devices  12.1 us (2%)
    psum x1, waiting for transfers between devices, per_device(): weight_sum, loss = lax.psum((weight_part, loss_part), ('lat', 'lon', 'ens'))  195 us
    all_gather x1, waiting for transfers between devices, per_device(): ensemble = lax.all_gather(response, 'ens', axis=0, tiled=True)  174 us
    add x32, other arithmetic, add_member(): return (pair_dist + distance, pair_slope + gap_value / distance)  141 us
    psum x1, blocking collectives, per_device(): weight_sum, loss = lax.psum((weight_part, loss_part), ('lat', 'lon', 'ens'))  73.8 us
    all_gather x1, waiting for transfers between devices, per_device(): whole_circle = lax.all_gather(extended, 'lon', axis=2, tiled=True)  19.3 us
    dot_general x3, matrix products, per_device(): jnp.einsum('objq,eobjc->eoqc', kernels, picked, preferred_element_type=jn...  19.3 us
  transfers between devices with their start and end apart: 8, of which 5 were waited for; matrix products, arithmetic and copies ran while one was open for 2% of the time, Pallas kernels for 0%

commit v1 on v0

--- a/solution.py
+++ b/solution.py
@@ -129,7 +129,7 @@
     weight_part = jnp.einsum(
         "eokjc,eojd->kcd", features, slopes, preferred_element_type=jnp.float32
     )
-    weight_sum, loss = lax.psum((weight_part, loss_part), ("lat", "lon", "ens"))
+    weight_sum, loss = lax.psum(lax.psum((weight_part, loss_part), "lat"), ("lon", "ens"))
     grad_weight = weight_sum * math.sqrt(weight.shape[0] * channels) / (lat_total * lon_total)
     feature_grad = jnp.einsum(
         "eojd,kcd->eokjc", slopes, weight, preferred_element_type=jnp.float32

time: 742 us -> 700 us (0.943)
  waiting for transfers between devices: 399 us -> 292 us
  blocking collectives: 73.8 us -> 138 us
    psum x1 -> x2, waiting for transfers between devices: 195 us -> 88.7 us  [the longest x1 70.1 us: per_device(): lax.psum(lax.psum((weight_part, loss_part), 'lat'), ('lon', 'ens'))]
    psum x1 -> x2, blocking collectives: 73.8 us -> 138 us  [the longest x1 128 us: per_device(): lax.psum(lax.psum((weight_part, loss_part), 'lat'), ('lon', 'ens'))]
  transfers between devices with their start and end apart: 8 -> 9, of which waited for: 5 -> 6; matrix products, arithmetic and copies ran while one was open for 2% -> 7% of each run, Pallas kernels for 0% -> 0%
where the time goes in v1:
time: 700 us; the launch traced here: 699 us
  waiting for transfers between devices  292 us (42%)
  other arithmetic  160 us (23%)
  blocking collectives  138 us (20%)
  matrix products  59.6 us (9%)
  local copies, waits for them, and re-layouts  22 us (3%)
  between operations  15.1 us (2%)
  starting transfers between devices  12.3 us (2%)
    all_gather x1, waiting for transfers between devices, per_device(): ensemble = lax.all_gather(response, 'ens', axis=0, tiled=True)  174 us
    add x32, other arithmetic, add_member(): return (pair_dist + distance, pair_slope + gap_value / distance)  142 us
    psum x1, blocking collectives, per_device(): lax.psum(lax.psum((weight_part, loss_part), 'lat'), ('lon', 'ens'))  128 us
    psum x1, waiting for transfers between devices, per_device(): lax.psum(lax.psum((weight_part, loss_part), 'lat'), ('lon', 'ens'))  70.1 us
    dot_general x3, matrix products, per_device(): jnp.einsum('objq,eobjc->eoqc', kernels, picked, preferred_element_type=jn...  19.3 us
    all_gather x1, waiting for transfers between devices, per_device(): whole_circle = lax.all_gather(extended, 'lon', axis=2, tiled=True)  19.3 us
    psum x1, waiting for transfers between devices, per_device(): lax.psum((weight_part, loss_part), 'lat')  18.5 us
  transfers between devices with their start and end apart: 9, of which 6 were waited for; matrix products, arithmetic and copies ran while one was open for 7% of the time, Pallas kernels for 0%

profile of v1, /device:TPU:2, one launch (start us, length us, event | category | flops | bytes accessed | tf_op | source)
XLA Modules:
  0.0 698.6 jit_solution(1935242484111782673)
XLA Ops:
  14.4 6.3 collective-permute-done
  27.0 19.3 %all-gather.4.cloned.1.call-done = bf16[1,4,1440,256]{3,2,1,0:T(8,128)(2,1)} async-done(((bf16[1,4,720,256]{3,2,1,0:T(8,128)(2,1)}), bf16[1,4,1440,256]{3,2,1,0:T(8,128)(2,1)}) %all-gather.4.cloned.1.call-update) | async-done | bytes 2949136 | tf_op jit(solution)/shard_map/all_gather | solution.py:96
  71.4 174.4 %all-gather.6.cloned.1.call-done = bf16[64,720,256]{2,1,0:T(8,128)(2,1)} async-done(((bf16[2,720,256]{2,1,0:T(8,128)(2,1)}), bf16[64,720,256]{2,1,0:T(8,128)(2,1)}) %all-gather.6.cloned.1.call-update) | async-done | bytes 23592976 | tf_op jit(solution)/shard_map/all_gather | solution.py:123
  245.8 142.3 %while.24 = (s32[]{:T(128)}, f32[1,2,720,256]{3,2,1,0:T(8,128)}, f32[1,2,720,256]{3,2,1,0:T(8,128)}, bf16[32,2,720,256]{3,2,1,0:T(8,128)(2,1)}, f32[1,2,720,256]{3,2,1,0:T(8,128)S(1)}, /*index=5*/s32[]{:T(128)}, s32[]{:T(128)}) while((s32[]{:T(128)}, f32[1,2,720,256]{3,2,1,0:T(8,128)}, f32[1,2,720,256]{3,2,1,0:T(8,128)}, ...), condition=%wide.region_1.2_spmd.clone, body=%wide.region_0.1_spmd.clone.sunk | while | flops 3317763 | bytes 8110179 | solution.py:74
  249.5 4.5 select_add_fusion.3
  253.9 4.5 select_add_fusion.3
  262.9 4.5 select_add_fusion.3
  267.4 4.5 select_add_fusion.3
  271.8 4.5 select_add_fusion.3
  276.3 4.5 select_add_fusion.3
  280.8 4.5 select_add_fusion.3
  285.3 4.5 select_add_fusion.3
  289.7 4.5 select_add_fusion.3
  294.2 4.5 select_add_fusion.3
  298.7 4.5 select_add_fusion.3
  303.2 4.5 select_add_fusion.3
  307.6 4.5 select_add_fusion.3
  312.1 4.5 select_add_fusion.3
  316.6 4.5 select_add_fusion.3
  325.5 4.5 select_add_fusion.3
  330.0 4.5 select_add_fusion.3
  392.1 6.4 convolution_bitcast_fusion.3
  408.1 5.7 fusion.12
  415.7 6.8 fusion.11
  422.5 6.8 fusion.10
  429.3 5.4 broadcast_in_dim.38
  434.7 8.8 %dynamic_update_slice.3 = f32[1,4,2880,256]{3,2,1,0:T(8,128)} dynamic-update-slice(f32[1,4,2880,256]{3,2,1,0:T(8,128)} %broadcast_in_dim.38, f32[1,4,752,256]{3,2,1,0:T(8,128)} %fusion.10, s32[]{:T(128)} %constant.322.clone.1, s32[]{:T(128)} %constant.322.clone.1, s32[]{:T(128)S(6)} %select_n.39, s32[]{:T(128)} %constant.322.clone.1) | dynamic-update-slice | bytes 6160388 | tf_op jit(solution)/shard_map/dynamic_update_slice | solution.py:174
  443.5 9.4 %fusion.3 = bf16[1,4,1440,256]{3,2,1,0:T(8,128)(2,1)} fusion(f32[1,4,2880,256]{3,2,1,0:T(8,128)} %dynamic_update_slice.3, f32[3,4,256]{2,0,1:T(4,128)S(1)} %fusion.41, f32[1,1440]{1,0:T(1,128)S(1)} %copy-done.9, f32[1,1440]{1,0:T(1,128)S(1)} %copy-done.11, f32[3]{0:T(128)S(1)} %copy-done.13), kind=kOutput, calls=%fused_computation.12 | convolution fusion | flops 57516480 | bytes 14769420 | tf_op jit(solution)/shard_map/pj,eprc->erjc/dot_general | solution.py:172
  453.1 18.5 %all-reduce.5.cloned.1.call-done = f32[9,256,256]{2,1,0:T(8,128)} async-done(((f32[9,256,256]{2,1,0:T(8,128)}), f32[9,256,256]{2,1,0:T(8,128)}) %all-reduce.5.cloned.1.call-update) | async-done | bytes 2359312 | tf_op jit(solution)/shard_map/psum | solution.py:132
  472.3 9.9 %psum.30 = f32[]{:T(128)} all-reduce(f32[]{:T(128)S(6)} %div.141), channel_id=1, replica_groups=mesh['lat'=4,'lon'=2,'ens'=32] {'lat'}, use_global_device_ids=true, to_apply=%region_9.10 | all-reduce | flops 1 | bytes 8 | tf_op jit(solution)/shard_map/psum | solution.py:132
  482.2 127.6 %psum.31 = f32[]{:T(128)} all-reduce(f32[]{:T(128)} %psum.30), channel_id=1, replica_groups=mesh['lat'=4,'lon'=2,'ens'=32] {'lon','ens'}, use_global_device_ids=true, to_apply=%region_10.11 | all-reduce | flops 1 | bytes 8 | tf_op jit(solution)/shard_map/psum | solution.py:132
  616.9 70.1 %all-reduce.7.cloned.1.call-done = f32[9,256,256]{2,1,0:T(8,128)} async-done(((f32[9,256,256]{2,1,0:T(8,128)}), f32[9,256,256]{2,1,0:T(8,128)}) %all-reduce.7.cloned.1.call-update) | async-done | bytes 2359312 | tf_op jit(solution)/shard_map/psum | solution.py:132
  (149 shorter events, 132.0 us)
Async XLA Ops:
  7.2 59.9 %copy-start = (bf16[9,256,256]{2,1,0:T(8,128)(2,1)S(1)}, bf16[9,256,256]{2,1,0:T(8,128)(2,1)}, u32[]{:S(2)}) copy-start(bf16[9,256,256]{2,1,0:T(8,128)(2,1)} %param.23) | copy-start | bytes 3538948
  7.2 19.2 %copy-start.14 = (s32[2]{0:T(128)S(1)}, s32[2]{0:T(128)}, u32[]{:S(2)}) copy-start(s32[2]{0:T(128)} %param.24) | copy-start | bytes 28
  7.2 39.0 %all-gather.4.cloned.1.call-start = ((), (), s32[]{:S(2)}) async-start(), calls=%async_computation.1 | async-start | bytes 4423680 | tf_op jit(solution)/shard_map/all_gather | solution.py:96
  8.5 12.2 %collective-permute-start = (bf16[1,1,720,256]{3,2,1,0:T(8,128)(2,1)S(1)}, bf16[1,1,720,256]{3,2,1,0:T(8,128)(2,1)S(1)}, u32[]{:S(2)}, u32[]{:S(2)}) collective-permute-start(bf16[1,1,720,256]{3,2,1,0:T(8,128)(2,1)S(1)} %get-tuple-element.236), channel_id=1, source_target_pairs={{0,64},{64,128},{128,192},{1,65},{65,129},{129,193},{2,66},{66,130... | collective-permute-start | bytes 1105928 | tf_op jit(solution)/shard_map/ppermute | solution.py:17
  11.9 11.9 %collective-permute-start.1 = (bf16[1,1,720,256]{3,2,1,0:T(8,128)(2,1)S(1)}, bf16[1,1,720,256]{3,2,1,0:T(8,128)(2,1)S(1)}, u32[]{:S(2)}, u32[]{:S(2)}) collective-permute-start(bf16[1,1,720,256]{3,2,1,0:T(8,128)(2,1)S(1)} %get-tuple-element.237), channel_id=1, source_target_pairs={{64,0},{128,64},{192,128},{65,1},{129,65},{193,129},{66,2},{130,66... | collective-permute-start | bytes 1105928 | tf_op jit(solution)/shard_map/ppermute | solution.py:20
  26.2 219.6 %all-gather.6.cloned.1.call-start = ((), (), s32[]{:S(2)}) async-start(), calls=%async_computation.5 | async-start | bytes 24330240 | tf_op jit(solution)/shard_map/all_gather | solution.py:123
  26.3 25.0 %copy-start.12 = (f32[3]{0:T(128)}, f32[3]{0:T(128)S(1)}, u32[]{:S(2)}) copy-start(f32[3]{0:T(128)S(1)} %pad.37.clone) | copy-start | bytes 40
  26.7 24.6 %copy-start.8 = (f32[1,1440]{1,0:T(1,128)}, f32[1,1440]{1,0:T(1,128)S(1)}, u32[]{:S(2)}) copy-start(f32[1,1440]{1,0:T(1,128)S(1)} %get-tuple-element.247) | copy-start | bytes 17284
  26.7 24.6 %copy-start.10 = (f32[1,1440]{1,0:T(1,128)}, f32[1,1440]{1,0:T(1,128)S(1)}, u32[]{:S(2)}) copy-start(f32[1,1440]{1,0:T(1,128)S(1)} %get-tuple-element.248) | copy-start | bytes 17284
  26.9 30.9 %copy-start.6 = (f32[720,752]{1,0:T(8,128)}, f32[720,752]{1,0:T(8,128)S(1)}, u32[]{:S(2)}) copy-start(f32[720,752]{1,0:T(8,128)S(1)} %subtract_convert_fusion) | copy-start | bytes 6497284
  46.2 3.3 copy-start.2
  64.3 2.8 copy-start.4
  69.9 401.7 %all-reduce.5.cloned.1.call-start = ((), (), s32[]{:S(2)}) async-start(), calls=%async_computation.3 | async-start | bytes 4718592 | tf_op jit(solution)/shard_map/psum | solution.py:132
  245.8 142.3 %copy-start.5 = (bf16[2,720,256]{2,1,0:T(8,128)(2,1)S(1)}, bf16[2,720,256]{2,1,0:T(8,128)(2,1)}, u32[]{:S(2)}) copy-start(bf16[2,720,256]{2,1,0:T(8,128)(2,1)} %bitcast_convert_fusion) | copy-start | bytes 2211844
  406.3 1.8 copy-start.7
  407.5 202.3 %reduce-scatter.2.cloned.1.call-start = ((), (), s32[]{:S(2)}) async-start(), calls=%async_computation.2 | async-start | bytes 4423680 | tf_op jit(solution)/shard_map/reduce_scatter | solution.py:176
  434.7 8.8 %copy-start.9 = (f32[1,1440]{1,0:T(1,128)S(1)}, f32[1,1440]{1,0:T(1,128)}, u32[]{:S(2)}) copy-start(f32[1,1440]{1,0:T(1,128)} %copy-done.8) | copy-start | bytes 17284
  434.7 8.8 %copy-start.11 = (f32[1,1440]{1,0:T(1,128)S(1)}, f32[1,1440]{1,0:T(1,128)}, u32[]{:S(2)}) copy-start(f32[1,1440]{1,0:T(1,128)} %copy-done.10) | copy-start | bytes 17284
  434.7 8.8 %copy-start.13 = (f32[3]{0:T(128)S(1)}, f32[3]{0:T(128)}, u32[]{:S(2)}) copy-start(f32[3]{0:T(128)} %copy-done.12) | copy-start | bytes 40
  453.0 234.0 %all-reduce.7.cloned.1.call-start = ((), (), s32[]{:S(2)}) async-start(), calls=%async_computation.4 | async-start | bytes 4718592 | tf_op jit(solution)/shard_map/psum | solution.py:132
  609.8 80.6 %copy-start.3 = (bf16[1,4,720,256]{3,2,1,0:T(8,128)(2,1)S(1)}, bf16[1,4,720,256]{3,2,1,0:T(8,128)(2,1)}, u32[]{:S(2)}) copy-start(bf16[1,4,720,256]{3,2,1,0:T(8,128)(2,1)} %reduce-scatter.2.cloned.1.call-done) | copy-start | bytes 4423684
  611.0 79.7 %collective-permute-start.2 = (bf16[1,1,720,256]{3,2,1,0:T(8,128)(2,1)S(1)}, bf16[1,1,720,256]{3,2,1,0:T(8,128)(2,1)S(1)}, u32[]{:S(2)}, u32[]{:S(2)}) collective-permute-start(bf16[1,1,720,256]{3,2,1,0:T(8,128)(2,1)S(1)} %get-tuple-element.234), channel_id=1, source_target_pairs={{0,64},{64,128},{128,192},{1,65},{65,129},{129,193},{2,66},{66,130... | collective-permute-start | bytes 1105928 | tf_op jit(solution)/shard_map/ppermute | solution.py:17
  613.0 77.8 %collective-permute-start.3 = (bf16[1,1,720,256]{3,2,1,0:T(8,128)(2,1)S(1)}, bf16[1,1,720,256]{3,2,1,0:T(8,128)(2,1)S(1)}, u32[]{:S(2)}, u32[]{:S(2)}) collective-permute-start(bf16[1,1,720,256]{3,2,1,0:T(8,128)(2,1)S(1)} %get-tuple-element.235), channel_id=1, source_target_pairs={{64,0},{128,64},{192,128},{65,1},{129,65},{193,129},{66,2},{130,66... | collective-permute-start | bytes 1105928 | tf_op jit(solution)/shard_map/ppermute | solution.py:20
  690.8 1.3 copy-start.1
Sparse Core Ops, SparseCore 0:
  26.4 19.8 all-gather.3
  70.0 175.7 all-gather.5
  407.6 63.9 all-reduce.4
  474.0 17.2 reduce-scatter.1
  494.5 192.4 all-reduce.6
